TPU v7x, 32 devices: a whole 2x2x4 slice. The times are simulated.
32 devices in a mesh: fsdp: 4 (over x, core), seq: 8 (over z, y).
Axes of the slice: x: 2, y: 2, z: 4, core: 2. Of those that a mesh axis runs over, the one named last changes fastest.
Arguments:
- tokens: bfloat16 [4, 56, 28, 512], P('fsdp', 'seq'), may hold values from -6 to 6
- cotangent: bfloat16 [4, 56, 28, 512], P('fsdp', 'seq'), may hold values from -6 to 6
- region_ids: int32 [56, 28], replicated, may hold values from 0 to 3
- relative_index: int32 [49, 49], replicated, may hold values from 0 to 168, as said below
- first_gain: bfloat16 [512], P('fsdp'), may hold values from 0.5 to 1.5
- first_offset: bfloat16 [512], P('fsdp'), may hold values from -3 to 3
- qkv_weight: bfloat16 [512, 1536], P('fsdp'), may hold values from -0.25 to 0.25
- proj_weight: bfloat16 [512, 512], P('fsdp'), may hold values from -0.75 to 0.75
- bias_table: bfloat16 [16, 169], P('fsdp'), may hold values from -4 to 4
- second_gain: bfloat16 [512], P('fsdp'), may hold values from 0.5 to 1.5
- second_offset: bfloat16 [512], P('fsdp'), may hold values from -3 to 3
- expand_weight: bfloat16 [512, 2048], P('fsdp'), may hold values from -0.25 to 0.25
- reduce_weight: bfloat16 [2048, 512], P('fsdp'), may hold values from -0.125 to 0.125
Outputs:
- output: bfloat16 [4, 56, 28, 512], P('fsdp', 'seq')
- tokens_grad: float32 [4, 56, 28, 512], P('fsdp', 'seq')
- first_gain_grad: float32 [512], P('fsdp')
- first_offset_grad: float32 [512], P('fsdp')
- qkv_weight_grad: float32 [512, 1536], P('fsdp')
- proj_weight_grad: float32 [512, 512], P('fsdp')
- bias_table_grad: float32 [16, 169], P('fsdp')
- second_gain_grad: float32 [512], P('fsdp')
- second_offset_grad: float32 [512], P('fsdp')
- expand_weight_grad: float32 [512, 2048], P('fsdp')
- reduce_weight_grad: float32 [2048, 512], P('fsdp')
Inputs may be any that keep to these rules, and one draw needn't show every extreme that they name: relative_index[i, j] depends only on the row and column offsets between positions i and j of a 7 x 7 window, and distinct offsets give distinct entries.
All inputs are finite; a program needn't handle non-finite values.
Results may differ from a plain program's by a relative error of at most 0.018.
Values may be sent and summed in bfloat16 or wider, within the bound.
A program may use at most 128 MiB of HBM per device.

v0:
```python
import jax
import jax.numpy as jnp
from jax import lax
from jax.sharding import PartitionSpec as P

WS = 7
SHIFT = 3
EPSILON = 1e-05
MASKED = -100.0
SQRT_HALF = 0.7071067811865476
INV_ROOT_TAU = 0.3989422804014327


def layer_norm(values, norm_gain, norm_offset):
    average = jnp.mean(values, axis=-1, keepdims=True)
    centred = values - average
    variance = jnp.mean(centred * centred, axis=-1, keepdims=True)
    inverse = lax.rsqrt(variance + EPSILON)
    normed = centred * inverse
    return (normed * norm_gain + norm_offset, normed, inverse)


def norm_back(upstream, normed, inverse, norm_gain):
    scaled = upstream * norm_gain
    mean_grad = jnp.mean(scaled, axis=-1, keepdims=True)
    second = jnp.mean(scaled * normed, axis=-1, keepdims=True)
    grad_in = inverse * (scaled - mean_grad - normed * second)
    lead_axes = tuple(range(upstream.ndim - 1))
    return (grad_in, jnp.sum(upstream * normed, axis=lead_axes), jnp.sum(upstream, axis=lead_axes))


def gelu_parts(hidden):
    normal_cdf = 0.5 * (1.0 + jax.scipy.special.erf(hidden * SQRT_HALF))
    density = jnp.exp(-0.5 * hidden * hidden) * INV_ROOT_TAU
    return (hidden * normal_cdf, normal_cdf + hidden * density)


def to_windows(field_in, num_heads):
    lead_dims = field_in.shape[:-3]
    num_rows, num_cols, features = field_in.shape[-3:]
    lead_count = len(lead_dims)
    pieces = field_in.reshape(
        lead_dims + (num_rows // WS, WS, num_cols // WS, WS, num_heads, features // num_heads)
    )
    axis_order = tuple(range(lead_count)) + (
        lead_count,
        lead_count + 2,
        lead_count + 4,
        lead_count + 1,
        lead_count + 3,
        lead_count + 5,
    )
    return pieces.transpose(axis_order).reshape(
        lead_dims + (num_rows // WS, num_cols // WS, num_heads, WS * WS, features // num_heads)
    )


def from_windows(window_tiles):
    lead_dims = window_tiles.shape[:-5]
    win_rows, win_cols, num_heads, positions, head_dim = window_tiles.shape[-5:]
    lead_count = len(lead_dims)
    pieces = window_tiles.reshape(lead_dims + (win_rows, win_cols, num_heads, WS, WS, head_dim))
    axis_order = tuple(range(lead_count)) + (
        lead_count,
        lead_count + 3,
        lead_count + 1,
        lead_count + 4,
        lead_count + 2,
        lead_count + 5,
    )
    return pieces.transpose(axis_order).reshape(
        lead_dims + (win_rows * WS, win_cols * WS, num_heads * head_dim)
    )


def make_mask(regions):
    num_rows, num_cols = regions.shape
    region_tiles = (
        regions.reshape(num_rows // WS, WS, num_cols // WS, WS)
        .transpose(0, 2, 1, 3)
        .reshape(num_rows // WS, num_cols // WS, WS * WS)
    )
    same_region = region_tiles[..., :, None] == region_tiles[..., None, :]
    return jnp.where(same_region, 0.0, MASKED).astype(jnp.float32)


def one_hot_index(relative_index, entries):
    return (relative_index[..., None] == jnp.arange(entries, dtype=jnp.int32)).astype(jnp.float32)


def table_bias(table_rows, relative_index):
    onehot = one_hot_index(relative_index, table_rows.shape[-1])
    return jnp.einsum("ijr,hr->hij", onehot, table_rows, precision=lax.Precision.HIGHEST)


def table_grad(bias_grad, relative_index, entries):
    onehot = one_hot_index(relative_index, entries)
    return jnp.einsum("hij,ijr->hr", bias_grad, onehot, precision=lax.Precision.HIGHEST)


def attend_forward(qkv_field, rel_bias, mask_add, num_heads):
    rolled = jnp.roll(qkv_field, -SHIFT, axis=-2)
    window_tiles = to_windows(rolled, num_heads)
    queries, key_tiles, value_tiles = (window_tiles[:, 0], window_tiles[:, 1], window_tiles[:, 2])
    scores = (
        jnp.einsum("bxyhid,bxyhjd->bxyhij", queries, key_tiles, preferred_element_type=jnp.float32)
        + rel_bias
        + mask_add[:, :, None]
    )
    exp_scores = jnp.exp(scores)
    row_total = jnp.sum(exp_scores, axis=-1, keepdims=True)
    attn_probs = (exp_scores / row_total).astype(jnp.bfloat16)
    attn_tiles = jnp.einsum(
        "bxyhij,bxyhjd->bxyhid", attn_probs, value_tiles, preferred_element_type=jnp.float32
    ).astype(jnp.bfloat16)
    field_out = jnp.roll(from_windows(attn_tiles), SHIFT, axis=-2)
    return (field_out, (queries, key_tiles, value_tiles, jnp.log(row_total)))


def attend_backward(grad_field, kept_state, rel_bias, mask_add, num_heads):
    queries, key_tiles, value_tiles, log_total = kept_state
    grad_tiles = to_windows(jnp.roll(grad_field, -SHIFT, axis=-2), num_heads)
    scores = (
        jnp.einsum("bxyhid,bxyhjd->bxyhij", queries, key_tiles, preferred_element_type=jnp.float32)
        + rel_bias
        + mask_add[:, :, None]
    )
    probs_back = jnp.exp(scores - log_total)
    value_grad = jnp.einsum(
        "bxyhij,bxyhid->bxyhjd",
        probs_back.astype(jnp.bfloat16),
        grad_tiles,
        preferred_element_type=jnp.float32,
    )
    prob_grad = jnp.einsum(
        "bxyhid,bxyhjd->bxyhij", grad_tiles, value_tiles, preferred_element_type=jnp.float32
    )
    score_grad = probs_back * (prob_grad - jnp.sum(probs_back * prob_grad, axis=-1, keepdims=True))
    score_low = score_grad.astype(jnp.bfloat16)
    query_scale = queries.shape[-1] ** (-0.5)
    query_grad = (
        jnp.einsum(
            "bxyhij,bxyhjd->bxyhid", score_low, key_tiles, preferred_element_type=jnp.float32
        )
        * query_scale
    )
    key_grad = jnp.einsum(
        "bxyhij,bxyhid->bxyhjd", score_low, queries, preferred_element_type=jnp.float32
    )
    stacked = jnp.stack([query_grad, key_grad, value_grad], axis=1).astype(jnp.bfloat16)
    field_grad = jnp.roll(from_windows(stacked), SHIFT, axis=-2)
    return (field_grad, jnp.sum(score_grad, axis=(0, 1, 2)))


def shards(
    tokens,
    cotangent,
    region_ids,
    relative_index,
    first_gain,
    first_offset,
    qkv_weight,
    proj_weight,
    bias_table,
    second_gain,
    second_offset,
    expand_weight,
    reduce_weight,
):
    gathered = (
        lax.all_gather(first_gain, "fsdp", axis=0, tiled=True),
        lax.all_gather(first_offset, "fsdp", axis=0, tiled=True),
        lax.all_gather(qkv_weight, "fsdp", axis=0, tiled=True),
        lax.all_gather(proj_weight, "fsdp", axis=0, tiled=True),
        lax.all_gather(bias_table, "fsdp", axis=0, tiled=True),
        lax.all_gather(second_gain, "fsdp", axis=0, tiled=True),
        lax.all_gather(second_offset, "fsdp", axis=0, tiled=True),
        lax.all_gather(expand_weight, "fsdp", axis=0, tiled=True),
        lax.all_gather(reduce_weight, "fsdp", axis=0, tiled=True),
    )
    gain_one = gathered[0].astype(jnp.float32)
    offset_one = gathered[1].astype(jnp.float32)
    qkv_full = gathered[2]
    proj_full = gathered[3]
    table_full = gathered[4].astype(jnp.float32)
    gain_two = gathered[5].astype(jnp.float32)
    offset_two = gathered[6].astype(jnp.float32)
    expand_full = gathered[7]
    reduce_full = gathered[8]
    num_images, num_rows, num_cols, width = tokens.shape
    num_heads, entries = table_full.shape
    query_scale = (width // num_heads) ** (-0.5)
    factors = jnp.array([query_scale, 1.0, 1.0], dtype=jnp.float32).reshape(1, 3, 1, 1, 1)
    qkv_cols = qkv_full.reshape(width, 3, width)
    inputs = tokens.astype(jnp.float32)
    normed_one, hat_one, inv_one = layer_norm(inputs, gain_one, offset_one)
    first_low = normed_one.astype(jnp.bfloat16)
    per_device = num_heads // lax.axis_size("seq")
    head_start = lax.axis_index("seq") * per_device
    qkv_local = (
        jnp.einsum("brwc,ctd->btrwd", first_low, qkv_cols, preferred_element_type=jnp.float32)
        * factors
    ).astype(jnp.bfloat16)
    qkv_heads = lax.all_to_all(qkv_local, "seq", split_axis=4, concat_axis=2, tiled=True)
    qkv_heads = jnp.roll(qkv_heads, -SHIFT, axis=2)
    rel_bias = table_bias(
        lax.dynamic_slice_in_dim(table_full, head_start, per_device, 0), relative_index
    )
    mask_add = make_mask(region_ids)
    attn_heads, kept_state = attend_forward(qkv_heads, rel_bias, mask_add, per_device)
    attn_heads = jnp.roll(attn_heads, SHIFT, axis=1)
    attended = lax.all_to_all(attn_heads, "seq", split_axis=1, concat_axis=3, tiled=True)
    middle = inputs + jnp.einsum(
        "brwc,cd->brwd", attended, proj_full, preferred_element_type=jnp.float32
    )
    normed_two, hat_two, inv_two = layer_norm(middle, gain_two, offset_two)
    second_low = normed_two.astype(jnp.bfloat16)
    hidden = jnp.einsum(
        "brwc,cf->brwf", second_low, expand_full, preferred_element_type=jnp.float32
    )
    activated, slope = gelu_parts(hidden)
    act_low = activated.astype(jnp.bfloat16)
    output = (
        middle
        + jnp.einsum("brwf,fc->brwc", act_low, reduce_full, preferred_element_type=jnp.float32)
    ).astype(jnp.bfloat16)
    reduce_grad = jnp.einsum(
        "brwf,brwc->fc", act_low, cotangent, preferred_element_type=jnp.float32
    )
    hidden_grad = (
        jnp.einsum("brwc,fc->brwf", cotangent, reduce_full, preferred_element_type=jnp.float32)
        * slope
    ).astype(jnp.bfloat16)
    expand_grad = jnp.einsum(
        "brwc,brwf->cf", second_low, hidden_grad, preferred_element_type=jnp.float32
    )
    upstream_two = jnp.einsum(
        "brwf,cf->brwc", hidden_grad, expand_full, preferred_element_type=jnp.float32
    )
    back_two, gain_two_grad, offset_two_grad = norm_back(upstream_two, hat_two, inv_two, gain_two)
    middle_grad = cotangent.astype(jnp.float32) + back_two
    middle_low = middle_grad.astype(jnp.bfloat16)
    proj_grad = jnp.einsum(
        "brwc,brwd->cd", attended, middle_low, preferred_element_type=jnp.float32
    )
    attended_grad = jnp.einsum(
        "brwd,cd->brwc", middle_low, proj_full, preferred_element_type=jnp.float32
    ).astype(jnp.bfloat16)
    grad_heads = lax.all_to_all(attended_grad, "seq", split_axis=3, concat_axis=1, tiled=True)
    grad_heads = jnp.roll(grad_heads, -SHIFT, axis=1)
    qkv_grad_heads, bias_grad = attend_backward(
        grad_heads, kept_state, rel_bias, mask_add, per_device
    )
    qkv_grad_heads = jnp.roll(qkv_grad_heads, SHIFT, axis=2)
    qkv_grad = lax.all_to_all(qkv_grad_heads, "seq", split_axis=2, concat_axis=4, tiled=True)
    table_part = table_grad(bias_grad, relative_index, entries)
    table_grads = lax.dynamic_update_slice(
        jnp.zeros((num_heads, entries), jnp.float32), table_part, (head_start, 0)
    )
    qkv_grad_w = jnp.einsum(
        "brwc,btrwd->ctd", first_low, qkv_grad, preferred_element_type=jnp.float32
    ).reshape(width, 3 * width)
    upstream_one = jnp.einsum(
        "btrwd,ctd->brwc", qkv_grad, qkv_cols, preferred_element_type=jnp.float32
    )
    back_one, gain_one_grad, offset_one_grad = norm_back(upstream_one, hat_one, inv_one, gain_one)
    tokens_grad = middle_grad + back_one
    shares = (
        lax.psum_scatter(
            gain_one_grad.astype(jnp.bfloat16), "fsdp", scatter_dimension=0, tiled=True
        ).astype(jnp.float32),
        lax.psum_scatter(
            offset_one_grad.astype(jnp.bfloat16), "fsdp", scatter_dimension=0, tiled=True
        ).astype(jnp.float32),
        lax.psum_scatter(
            qkv_grad_w.astype(jnp.bfloat16), "fsdp", scatter_dimension=0, tiled=True
        ).astype(jnp.float32),
        lax.psum_scatter(
            proj_grad.astype(jnp.bfloat16), "fsdp", scatter_dimension=0, tiled=True
        ).astype(jnp.float32),
        lax.psum_scatter(
            table_grads.astype(jnp.bfloat16), "fsdp", scatter_dimension=0, tiled=True
        ).astype(jnp.float32),
        lax.psum_scatter(
            gain_two_grad.astype(jnp.bfloat16), "fsdp", scatter_dimension=0, tiled=True
        ).astype(jnp.float32),
        lax.psum_scatter(
            offset_two_grad.astype(jnp.bfloat16), "fsdp", scatter_dimension=0, tiled=True
        ).astype(jnp.float32),
        lax.psum_scatter(
            expand_grad.astype(jnp.bfloat16), "fsdp", scatter_dimension=0, tiled=True
        ).astype(jnp.float32),
        lax.psum_scatter(
            reduce_grad.astype(jnp.bfloat16), "fsdp", scatter_dimension=0, tiled=True
        ).astype(jnp.float32),
    )
    totals = (
        lax.psum(shares[0].astype(jnp.bfloat16), "seq").astype(jnp.float32),
        lax.psum(shares[1].astype(jnp.bfloat16), "seq").astype(jnp.float32),
        lax.psum(shares[2].astype(jnp.bfloat16), "seq").astype(jnp.float32),
        lax.psum(shares[3].astype(jnp.bfloat16), "seq").astype(jnp.float32),
        lax.psum(shares[4].astype(jnp.bfloat16), "seq").astype(jnp.float32),
        lax.psum(shares[5].astype(jnp.bfloat16), "seq").astype(jnp.float32),
        lax.psum(shares[6].astype(jnp.bfloat16), "seq").astype(jnp.float32),
        lax.psum(shares[7].astype(jnp.bfloat16), "seq").astype(jnp.float32),
        lax.psum(shares[8].astype(jnp.bfloat16), "seq").astype(jnp.float32),
    )
    qkv_total = totals[2]
    proj_total = totals[3]
    expand_total = totals[7]
    reduce_total = totals[8]
    return (
        output,
        tokens_grad,
        totals[0],
        totals[1],
        qkv_total,
        proj_total,
        totals[4],
        totals[5],
        totals[6],
        expand_total,
        reduce_total,
    )


def solution(mesh):
    placed = (
        P("fsdp", "seq", None, None),
        P("fsdp", "seq", None, None),
        P(),
        P(),
        P("fsdp"),
        P("fsdp"),
        P("fsdp", None),
        P("fsdp", None),
        P("fsdp", None),
        P("fsdp"),
        P("fsdp"),
        P("fsdp", None),
        P("fsdp", None),
    )
    return jax.shard_map(
        shards,
        mesh=mesh,
        in_specs=placed,
        out_specs=(
            P("fsdp", "seq", None, None),
            P("fsdp", "seq", None, None),
            P("fsdp"),
            P("fsdp"),
            P("fsdp", None),
            P("fsdp", None),
            P("fsdp", None),
            P("fsdp"),
            P("fsdp"),
            P("fsdp", None),
            P("fsdp", None),
        ),
        check_vma=False,
    )
```

profile of v0, /device:TPU:0, one launch (start us, length us, event | category | flops | bytes accessed | tf_op | source)
XLA Modules:
  0.0 359.1 jit_solution(13753991665746310214)
XLA Ops:
  10.0 6.2 %all-gather = bf16[4,1,128]{2,1,0:T(2,128)(2,1)S(1)} all-gather(bf16[1,1,128]{2,1,0:T(2,128)(2,1)} %bitcast.275), channel_id=1, replica_groups=mesh['fsdp'=4,'seq'=8] {'fsdp'}, dimensions={0}, use_global_device_ids=true | all-gather | bytes 1280 | tf_op jit(solution)/shard_map/all_gather | solution.py:171
  16.2 5.4 %all-gather.1 = bf16[4,1,128]{2,1,0:T(2,128)(2,1)S(1)} all-gather(bf16[1,1,128]{2,1,0:T(2,128)(2,1)} %bitcast.276), channel_id=1, replica_groups=mesh['fsdp'=4,'seq'=8] {'fsdp'}, dimensions={0}, use_global_device_ids=true | all-gather | bytes 1280 | tf_op jit(solution)/shard_map/all_gather | solution.py:172
  22.0 10.7 %all-gather.9.cloned.1.call-done = bf16[512,1536]{0,1:T(8,128)(2,1)} async-done(((bf16[128,1536]{0,1:T(8,128)(2,1)}), bf16[512,1536]{0,1:T(8,128)(2,1)}) %all-gather.9.cloned.1.call-update) | async-done | bytes 1572880 | tf_op jit(solution)/shard_map/all_gather | solution.py:173
  32.7 2.9 fusion.22
  35.6 3.7 %copy.100 = bf16[1,3,7,28,512]{3,2,1,0,4:T(8,128)(2,1)S(1)} copy(bf16[1,3,7,28,512]{4,3,1,2,0:T(8,128)(2,1)} %fusion.22) | data formatting | bytes 1204224 | tf_op jit(solution)/shard_map/convert_element_type | solution.py:203
  39.4 4.6 %reshape.406 = bf16[8,2,18816]{2,1,0:T(2,128)(2,1)} reshape(bf16[512,1,3,7,28]{4,3,2,1,0:T(8,128)(2,1)S(1)} %bitcast.239) | data formatting | bytes 1204224
  44.0 5.6 %all-to-all-start = ((bf16[8,2,18816]{2,1,0:T(2,128)(2,1)}), bf16[8,2,18816]{2,1,0:T(2,128)(2,1)}, u32[]{:S(2)}, u32[]{:S(2)}) async-start(bf16[8,2,18816]{2,1,0:T(2,128)(2,1)} %reshape.406), calls=%async_computation | async-start | bytes 1204224 | tf_op jit(solution)/shard_map/all_to_all | solution.py:204
  50.4 5.4 %all-gather.2 = bf16[4,4,169]{2,1,0:T(4,128)(2,1)S(1)} all-gather(bf16[1,4,169]{2,1,0:T(4,128)(2,1)S(1)} %bitcast.272), channel_id=1, replica_groups=mesh['fsdp'=4,'seq'=8] {'fsdp'}, dimensions={0}, use_global_device_ids=true | all-gather | bytes 6760 | tf_op jit(solution)/shard_map/all_gather | solution.py:175
  58.4 7.9 %all-to-all-done = bf16[8,2,18816]{2,1,0:T(2,128)(2,1)} async-done(((bf16[8,2,18816]{2,1,0:T(2,128)(2,1)}), bf16[8,2,18816]{2,1,0:T(2,128)(2,1)}, u32[]{:S(2)}, u32[]{:S(2)}) %all-to-all-start) | async-done | bytes 602144 | tf_op jit(solution)/shard_map/all_to_all | solution.py:204
  66.3 5.0 %reshape.407 = bf16[512,1,3,7,28]{4,3,2,1,0:T(8,128)(2,1)S(1)} reshape(bf16[8,2,18816]{2,1,0:T(2,128)(2,1)} %all-to-all-done) | data formatting | bytes 1204224
  71.3 4.5 %copy.101 = bf16[1,3,7,28,8,64]{5,2,4,3,1,0:T(8,128)(2,1)} copy(bf16[1,3,7,28,8,64]{3,2,1,5,4,0:T(8,128)(2,1)S(1)} %bitcast.238) | data formatting | bytes 1204224 | tf_op jit(solution)/shard_map/all_to_all | solution.py:204
  75.8 2.4 all_to_all.51
  80.4 4.3 %reshape.357 = bf16[1,3,8,7,4,7,2,32]{7,6,3,2,5,4,1,0:T(2,128)(2,1)S(1)} reshape(bf16[1,3,56,28,64]{4,2,3,1,0:T(8,128)(2,1)} %fusion.27) | data formatting | bytes 1204224 | tf_op jit(solution)/shard_map/reshape | solution.py:42
  98.7 3.7 %all-to-all-start.1 = ((bf16[8,2,6272]{2,1,0:T(2,128)(2,1)}), bf16[8,2,6272]{2,1,0:T(2,128)(2,1)S(1)}, u32[]{:S(2)}, u32[]{:S(2)}) async-start(bf16[8,2,6272]{2,1,0:T(2,128)(2,1)} %reshape.408), calls=%async_computation.1 | async-start | bytes 401408 | tf_op jit(solution)/shard_map/all_to_all | solution.py:212
  102.4 5.1 %all-gather.3 = bf16[4,1,128]{2,1,0:T(2,128)(2,1)S(1)} all-gather(bf16[1,1,128]{2,1,0:T(2,128)(2,1)S(1)} %bitcast.277), channel_id=1, replica_groups=mesh['fsdp'=4,'seq'=8] {'fsdp'}, dimensions={0}, use_global_device_ids=true | all-gather | bytes 1280 | tf_op jit(solution)/shard_map/all_gather | solution.py:176
  107.4 5.0 %all-gather.4 = bf16[4,1,128]{2,1,0:T(2,128)(2,1)S(1)} all-gather(bf16[1,1,128]{2,1,0:T(2,128)(2,1)S(1)} %bitcast.278), channel_id=1, replica_groups=mesh['fsdp'=4,'seq'=8] {'fsdp'}, dimensions={0}, use_global_device_ids=true | all-gather | bytes 1280 | tf_op jit(solution)/shard_map/all_gather | solution.py:177
  112.5 7.9 %all_gather.31 = bf16[512,512]{1,0:T(8,128)(2,1)S(1)} all-gather(bf16[128,512]{1,0:T(8,128)(2,1)S(1)} %copy-done.22), channel_id=1, replica_groups=mesh['fsdp'=4,'seq'=8] {'fsdp'}, dimensions={0}, use_global_device_ids=true | all-gather | bytes 655360 | tf_op jit(solution)/shard_map/all_gather | solution.py:174
  121.9 4.0 %multiply_convert_fusion = (bf16[7,28,2048]{2,1,0:T(8,128)(2,1)}, f32[7,28,2048]{2,1,0:T(8,128)}) fusion(bf16[512,2048]{1,0:T(8,128)(2,1)} %all-gather.11.cloned.1.call-done, f32[1,7,28,512]{3,2,1,0:T(8,128)S(1)} %get-tuple-element.85, f32[512]{0:T(512)S(1)} %bitcast.270, f32[512]{0:T(512)S(1)} %bitcast.260, f32[7,28]{1,0:T(8,128)S(1)} %add_rsqrt_fusion, ...), kind=kOutput, calls=%fused_computation.25 | convolution fusion | flops 413550592 | bytes 4912672 | tf_op jit(solution)/shard_map/brwc,cf->brwf/dot_general | solution.py:218
  125.9 3.3 fusion.3
  132.7 3.4 bitcast_convert_fusion.1
  137.0 3.3 bitcast_convert_fusion
  145.0 5.9 %all-to-all-start.2 = ((bf16[8,2,6272]{2,1,0:T(2,128)(2,1)}), bf16[8,2,6272]{2,1,0:T(2,128)(2,1)S(1)}, u32[]{:S(2)}, u32[]{:S(2)}) async-start(bf16[8,2,6272]{2,1,0:T(2,128)(2,1)} %reshape.410), calls=%async_computation.2 | async-start | bytes 401408 | tf_op jit(solution)/shard_map/all_to_all | solution.py:249
  152.6 6.9 %all-to-all-done.2 = bf16[8,2,6272]{2,1,0:T(2,128)(2,1)S(1)} async-done(((bf16[8,2,6272]{2,1,0:T(2,128)(2,1)}), bf16[8,2,6272]{2,1,0:T(2,128)(2,1)S(1)}, u32[]{:S(2)}, u32[]{:S(2)}) %all-to-all-start.2) | async-done | bytes 200736 | tf_op jit(solution)/shard_map/all_to_all | solution.py:249
  168.6 2.4 copy.126
  180.3 2.3 reshape.371
  185.5 19.8 %all_to_all.66 = bf16[8,2,18816]{2,1,0:T(2,128)(2,1)S(1)} all-to-all(bf16[8,2,18816]{2,1,0:T(2,128)(2,1)S(1)} %reshape.412), channel_id=1, replica_groups=mesh['fsdp'=4,'seq'=8] {'seq'}, dimensions={0} | all-to-all | bytes 1204224 | tf_op jit(solution)/shard_map/all_to_all | solution.py:255
  213.1 9.0 %reduce-scatter.11.cloned.1.call-done = bf16[512,512]{1,0:T(8,128)(2,1)} async-done(((bf16[2048,512]{1,0:T(8,128)(2,1)}), bf16[512,512]{1,0:T(8,128)(2,1)}) %reduce-scatter.11.cloned.1.call-update) | async-done | bytes 524304 | tf_op jit(solution)/shard_map/reduce_scatter | solution.py:293
  222.1 30.6 %reduce-scatter.5.cloned.1.call-done = bf16[128,1536]{1,0:T(8,128)(2,1)} async-done(((bf16[512,1536]{1,0:T(8,128)(2,1)}), bf16[128,1536]{1,0:T(8,128)(2,1)}) %reduce-scatter.5.cloned.1.call-update) | async-done | bytes 393232 | tf_op jit(solution)/shard_map/reduce_scatter | solution.py:275
  252.7 2.9 fusion.32
  259.1 10.5 %all-reduce.7 = (bf16[512]{0:T(512)(128)(2,1)S(1)}, bf16[512]{0:T(512)(128)(2,1)S(1)}, bf16[16,169]{1,0:T(8,128)(2,1)S(1)}, bf16[512]{0:T(512)(128)(2,1)S(1)}, bf16[512]{0:T(512)(128)(2,1)S(1)}) all-reduce(bf16[512]{0:T(512)(128)(2,1)S(1)} %get-tuple-element.57, ...), channel_id=2, replica_groups=mesh['fsdp'=4,'seq'=8] {'fsdp'}, use_global_device_ids=true, to_apply=%region_11.12.clone | all-reduce | flops 4752 | bytes 19008
  270.0 21.9 %all-reduce.5 = (bf16[128]{0:T(256)(128)(2,1)S(1)}, bf16[128]{0:T(256)(128)(2,1)S(1)}, bf16[4,169]{1,0:T(4,128)(2,1)S(1)}, bf16[128]{0:T(256)(128)(2,1)S(1)}, bf16[128]{0:T(256)(128)(2,1)S(1)}) all-reduce(bf16[128]{0:T(256)(128)(2,1)S(1)} %dynamic-slice.1, ...), channel_id=1, replica_groups=mesh['fsdp'=4,'seq'=8] {'seq'}, use_global_device_ids=true, to_apply=%region_12.13 | all-reduce | flops 1188 | bytes 4752 | tf_op jit(solution)/shard_map/psum | solution.py:298
  295.9 50.3 %all-reduce.10.cloned.1.call-done = (bf16[128,1536]{1,0:T(8,128)(2,1)}, bf16[128,512]{1,0:T(8,128)(2,1)}, bf16[128,2048]{1,0:T(8,128)(2,1)}, bf16[512,512]{1,0:T(8,128)(2,1)}) async-done(((bf16[128,1536]{1,0:T(8,128)(2,1)}, bf16[128,512]{1,0:T(8,128)(2,1)}, bf16[128,2048]{1,0:T(8,128)(2,1)}, bf16[512,512]{1,0:T(8,128)(2,1)}), (bf16[128,1536]{1,0:T(8,128)(2,1)}, bf16[128,512]{1,0:T(8,128)(2,1)}, ...) | async-done | bytes 1572880 | tf_op jit(solution)/shard_map/psum | solution.py:300
  (202 shorter events, 75.8 us)
Async XLA Ops:
  7.2 25.5 %copy-start.34 = (f32[3]{0:T(128)S(1)}, f32[3]{0:T(128)}, u32[]{:S(2)}) copy-start(f32[3]{0:T(128)} %constant.41.clone) | copy-start | bytes 40
  7.2 14.5 %copy-start.7 = (bf16[1,7,28,512]{3,2,1,0:T(8,128)(2,1)S(1)}, bf16[1,7,28,512]{3,2,1,0:T(8,128)(2,1)}, u32[]{:S(2)}) copy-start(bf16[1,7,28,512]{3,2,1,0:T(8,128)(2,1)} %param.14) | copy-start | bytes 602116
  7.2 25.5 %all-gather.9.cloned.1.call-start = ((), (), s32[]{:S(2)}) async-start(), calls=%async_computation.8 | async-start | bytes 1966080 | tf_op jit(solution)/shard_map/all_gather | solution.py:173
  9.2 112.7 %all-gather.11.cloned.1.call-start = ((), (), s32[]{:S(2)}) async-start(), calls=%async_computation.9 | async-start | bytes 2621440 | tf_op jit(solution)/shard_map/all_gather | solution.py:178
  21.6 11.1 %copy-start.26 = (f32[4,1,128]{2,1,0:T(1,128)}, f32[4,1,128]{2,1,0:T(1,128)S(1)}, u32[]{:S(2)}) copy-start(f32[4,1,128]{2,1,0:T(1,128)S(1)} %convert_element_type.190) | copy-start | bytes 6148
  39.4 11.0 %copy-start.25 = (bf16[4,169]{1,0:T(4,128)(2,1)S(1)}, bf16[4,169]{1,0:T(4,128)(2,1)}, u32[]{:S(2)}) copy-start(bf16[4,169]{1,0:T(4,128)(2,1)} %param.22) | copy-start | bytes 4060
  39.4 16.4 %copy-start.31 = (s32[49,49]{1,0:T(8,128)S(1)}, s32[49,49]{1,0:T(8,128)}, u32[]{:S(2)}) copy-start(s32[49,49]{1,0:T(8,128)} %param.17) | copy-start | bytes 28816
  44.0 12.7 %copy-start.23 = (s32[56,28]{0,1:T(8,128)S(1)}, s32[56,28]{0,1:T(8,128)}, u32[]{:S(2)}) copy-start(s32[56,28]{0,1:T(8,128)} %param.16) | copy-start | bytes 18820
  44.0 22.3 %all-to-all-start = ((bf16[8,2,18816]{2,1,0:T(2,128)(2,1)}), bf16[8,2,18816]{2,1,0:T(2,128)(2,1)}, u32[]{:S(2)}, u32[]{:S(2)}) async-start(bf16[8,2,18816]{2,1,0:T(2,128)(2,1)} %reshape.406), calls=%async_computation | async-start | bytes 1204224 | tf_op jit(solution)/shard_map/all_to_all | solution.py:204
  49.6 76.3 %all-gather.13.cloned.1.call-start = ((), (), s32[]{:S(2)}) async-start(), calls=%async_computation.10 | async-start | bytes 2621440 | tf_op jit(solution)/shard_map/all_gather | solution.py:179
  97.4 5.0 %copy-start.29 = (bf16[128]{0:T(256)(128)(2,1)S(1)}, bf16[128]{0:T(256)(128)(2,1)}, u32[]{:S(2)}) copy-start(bf16[128]{0:T(256)(128)(2,1)} %param.23) | copy-start | bytes 772
  97.4 10.1 %copy-start.30 = (bf16[128]{0:T(256)(128)(2,1)S(1)}, bf16[128]{0:T(256)(128)(2,1)}, u32[]{:S(2)}) copy-start(bf16[128]{0:T(256)(128)(2,1)} %param.24) | copy-start | bytes 772
  97.4 15.1 %copy-start.22 = (bf16[128,512]{1,0:T(8,128)(2,1)S(1)}, bf16[128,512]{1,0:T(8,128)(2,1)}, u32[]{:S(2)}) copy-start(bf16[128,512]{1,0:T(8,128)(2,1)} %param.21) | copy-start | bytes 393220
  98.7 21.8 %all-to-all-start.1 = ((bf16[8,2,6272]{2,1,0:T(2,128)(2,1)}), bf16[8,2,6272]{2,1,0:T(2,128)(2,1)S(1)}, u32[]{:S(2)}, u32[]{:S(2)}) async-start(bf16[8,2,6272]{2,1,0:T(2,128)(2,1)} %reshape.408), calls=%async_computation.1 | async-start | bytes 401408 | tf_op jit(solution)/shard_map/all_to_all | solution.py:212
  102.3 110.7 %reduce-scatter.7.cloned.1.call-start = ((), (), s32[]{:S(2)}) async-start(), calls=%async_computation.12 | async-start | bytes 655360 | tf_op jit(solution)/shard_map/reduce_scatter | solution.py:278
  112.5 8.8 %copy-start.8 = (bf16[1,7,28,512]{3,2,1,0:T(8,128)(2,1)S(1)}, bf16[1,7,28,512]{3,2,1,0:T(8,128)(2,1)}, u32[]{:S(2)}) copy-start(bf16[1,7,28,512]{3,2,1,0:T(8,128)(2,1)} %param.14) | copy-start | bytes 602116
  121.9 4.0 %copy-start.18 = (bf16[1,7,28,512]{3,2,1,0:T(8,128)(2,1)S(1)}, bf16[1,7,28,512]{3,2,1,0:T(8,128)(2,1)}, u32[]{:S(2)}) copy-start(bf16[1,7,28,512]{3,2,1,0:T(8,128)(2,1)} %param.15) | copy-start | bytes 602116
  125.9 3.3 copy-start.12
  131.5 8.8 %copy-start.4 = (f32[1,7,28,512]{3,2,1,0:T(8,128)}, f32[1,7,28,512]{3,2,1,0:T(8,128)S(1)}, u32[]{:S(2)}) copy-start(f32[1,7,28,512]{3,2,1,0:T(8,128)S(1)} %fusion.67) | copy-start | bytes 1204228
  132.7 80.4 %reduce-scatter.9.cloned.1.call-start = ((), (), s32[]{:S(2)}) async-start(), calls=%async_computation.13 | async-start | bytes 2621440 | tf_op jit(solution)/shard_map/reduce_scatter | solution.py:290
  136.1 86.0 %reduce-scatter.11.cloned.1.call-start = ((), (), s32[]{:S(2)}) async-start(), calls=%async_computation.14 | async-start | bytes 2621440 | tf_op jit(solution)/shard_map/reduce_scatter | solution.py:293
  145.0 14.5 %all-to-all-start.2 = ((bf16[8,2,6272]{2,1,0:T(2,128)(2,1)}), bf16[8,2,6272]{2,1,0:T(2,128)(2,1)S(1)}, u32[]{:S(2)}, u32[]{:S(2)}) async-start(bf16[8,2,6272]{2,1,0:T(2,128)(2,1)} %reshape.410), calls=%async_computation.2 | async-start | bytes 401408 | tf_op jit(solution)/shard_map/all_to_all | solution.py:249
  150.9 101.7 %reduce-scatter.5.cloned.1.call-start = ((), (), s32[]{:S(2)}) async-start(), calls=%async_computation.11 | async-start | bytes 1966080 | tf_op jit(solution)/shard_map/reduce_scatter | solution.py:275
  164.1 3.1 copy-start.15
  167.2 3.8 %copy-start.14 = (bf16[1,1,8,4,2,49,32]{5,6,4,3,2,1,0:T(8,128)(2,1)S(1)}, bf16[1,1,8,4,2,49,32]{5,6,4,3,2,1,0:T(8,128)(2,1)}, u32[]{:S(2)}) copy-start(bf16[1,1,8,4,2,49,32]{5,6,4,3,2,1,0:T(8,128)(2,1)} %copy.151) | copy-start | bytes 602116
  174.8 3.1 copy-start.10
  211.1 41.6 %copy-start.6 = (bf16[7,28,2048]{2,1,0:T(8,128)(2,1)S(1)}, bf16[7,28,2048]{2,1,0:T(8,128)(2,1)}, u32[]{:S(2)}) copy-start(bf16[7,28,2048]{2,1,0:T(8,128)(2,1)} %get-tuple-element.86) | copy-start | bytes 2408452
  211.1 135.1 %all-reduce.10.cloned.1.call-start = ((), (), s32[]{:S(2)}) async-start(), calls=%async_computation.15 | async-start | bytes 3145728 | tf_op jit(solution)/shard_map/psum | solution.py:300
  252.7 3.1 copy-start.32
  256.9 37.6 %copy-start.5 = (f32[1,7,28,512]{3,2,1,0:T(8,128)S(1)}, f32[1,7,28,512]{3,2,1,0:T(8,128)}, u32[]{:S(2)}) copy-start(f32[1,7,28,512]{3,2,1,0:T(8,128)} %copy-done.4) | copy-start | bytes 1204228
  346.2 3.7 %copy-start.17 = (bf16[128,2048]{1,0:T(8,128)(2,1)S(1)}, bf16[128,2048]{1,0:T(8,128)(2,1)}, u32[]{:S(2)}) copy-start(bf16[128,2048]{1,0:T(8,128)(2,1)} %get-tuple-element.70) | copy-start | bytes 1572868
  346.2 4.7 %copy-start.16 = (bf16[512,512]{1,0:T(8,128)(2,1)S(1)}, bf16[512,512]{1,0:T(8,128)(2,1)}, u32[]{:S(2)}) copy-start(bf16[512,512]{1,0:T(8,128)(2,1)} %get-tuple-element.71) | copy-start | bytes 1572868
  (17 other events, 29.5 us)
Sparse Core Ops, SparseCore 0:
  10.1 22.5 all-gather.8
  34.3 22.5 all-gather.10
  58.5 22.5 all-gather.12
  132.8 22.0 reduce-scatter.6
  157.2 31.1 reduce-scatter.8
  190.8 31.1 reduce-scatter.10
  224.6 28.0 reduce-scatter.4
  256.5 89.6 all-reduce.9
where the time goes:
time: 364 us; the launch traced here: 359 us
  waiting for transfers between devices  117 us (32%)
  blocking collectives  87.2 us (24%)
  local copies, waits for them, and re-layouts  70.8 us (19%)
  matrix products  37 us (10%)
  between operations  16.5 us (5%)
  starting transfers between devices  15.7 us (4%)
  other arithmetic  15.1 us (4%)
    psum x1, waiting for transfers between devices, shards(): lax.psum(shares[2].astype(jnp.bfloat16), 'seq').astype(jnp.float32)  50.3 us
    reduce_scatter x1, waiting for transfers between devices, shards(): lax.psum_scatter(qkv_grad_w.astype(jnp.bfloat16), 'fsdp', scatter_dimensi...  30.6 us
    unnamed x92, local copies, waits for them, and re-layouts  24.5 us
    psum x1, blocking collectives, shards(): lax.psum(shares[0].astype(jnp.bfloat16), 'seq').astype(jnp.float32)  21.9 us
    all_to_all x1, blocking collectives, shards(): lax.all_to_all(qkv_grad_heads, 'seq', split_axis=2, concat_axis=4, tiled=...  19.8 us
    all_gather x1, waiting for transfers between devices, shards(): lax.all_gather(qkv_weight, 'fsdp', axis=0, tiled=True)  10.7 us
    unnamed x1, blocking collectives  10.5 us
    reduce_scatter x1, waiting for transfers between devices, shards(): lax.psum_scatter(reduce_grad.astype(jnp.bfloat16), 'fsdp', scatter_dimens...  8.96 us
  transfers between devices with their start and end apart: 11, of which 6 were waited for; matrix products, arithmetic and copies ran while one was open for 28% of the time, Pallas kernels for 0%

commit v1 on v0

--- a/solution.py
+++ b/solution.py
@@ -295,7 +295,7 @@
         ).astype(jnp.float32),
     )
     totals = (
-        lax.psum(shares[0].astype(jnp.bfloat16), "seq").astype(jnp.float32),
+        jnp.sum(lax.all_gather(shares[0].astype(jnp.bfloat16), "seq"), axis=0).astype(jnp.float32),
         lax.psum(shares[1].astype(jnp.bfloat16), "seq").astype(jnp.float32),
         lax.psum(shares[2].astype(jnp.bfloat16), "seq").astype(jnp.float32),
         lax.psum(shares[3].astype(jnp.bfloat16), "seq").astype(jnp.float32),

time: 364 us -> 364 us (level)
  waiting for transfers between devices: 117 us -> 100 us
  blocking collectives: 87.2 us -> 104 us
    all_gather x0 -> x1, blocking collectives: none -> 16.3 us  [shards(): lax.all_gather(shares[0].astype(jnp.bfloat16), 'seq')]
    psum x1, waiting for transfers between devices: 50.3 us -> 36.9 us  [shards(): lax.psum(shares[2].astype(jnp.bfloat16), 'seq').astype(jnp.float32)]
where the time goes in v1:
time: 364 us; the launch traced here: 359 us
  blocking collectives  104 us (29%)
  waiting for transfers between devices  100 us (27%)
  local copies, waits for them, and re-layouts  70.8 us (19%)
  matrix products  37 us (10%)
  between operations  16.5 us (5%)
  starting transfers between devices  15.7 us (4%)
  other arithmetic  15.1 us (4%)
    psum x1, waiting for transfers between devices, shards(): lax.psum(shares[2].astype(jnp.bfloat16), 'seq').astype(jnp.float32)  36.9 us
    reduce_scatter x1, waiting for transfers between devices, shards(): lax.psum_scatter(qkv_grad_w.astype(jnp.bfloat16), 'fsdp', scatter_dimensi...  30.6 us
    unnamed x92, local copies, waits for them, and re-layouts  24.5 us
    psum x1, blocking collectives, shards(): lax.psum(shares[1].astype(jnp.bfloat16), 'seq').astype(jnp.float32)  22.5 us
    all_to_all x1, blocking collectives, shards(): lax.all_to_all(qkv_grad_heads, 'seq', split_axis=2, concat_axis=4, tiled=...  19.8 us
    all_gather x1, blocking collectives, shards(): lax.all_gather(shares[0].astype(jnp.bfloat16), 'seq')  16.3 us
    all_gather x1, waiting for transfers between devices, shards(): lax.all_gather(qkv_weight, 'fsdp', axis=0, tiled=True)  10.7 us
    unnamed x1, blocking collectives  10.1 us
  transfers between devices with their start and end apart: 11, of which 6 were waited for; matrix products, arithmetic and copies ran while one was open for 28% of the time, Pallas kernels for 0%

profile of v1, /device:TPU:0, one launch (start us, length us, event | category | flops | bytes accessed | tf_op | source)
XLA Modules:
  0.0 359.1 jit_solution(7324376830466959199)
XLA Ops:
  10.0 6.2 %all-gather.1 = bf16[4,1,128]{2,1,0:T(2,128)(2,1)S(1)} all-gather(bf16[1,1,128]{2,1,0:T(2,128)(2,1)} %bitcast.277), channel_id=1, replica_groups=mesh['fsdp'=4,'seq'=8] {'fsdp'}, dimensions={0}, use_global_device_ids=true | all-gather | bytes 1280 | tf_op jit(solution)/shard_map/all_gather | solution.py:171
  16.2 5.4 %all-gather.2 = bf16[4,1,128]{2,1,0:T(2,128)(2,1)S(1)} all-gather(bf16[1,1,128]{2,1,0:T(2,128)(2,1)} %bitcast.278), channel_id=1, replica_groups=mesh['fsdp'=4,'seq'=8] {'fsdp'}, dimensions={0}, use_global_device_ids=true | all-gather | bytes 1280 | tf_op jit(solution)/shard_map/all_gather | solution.py:172
  22.0 10.7 %all-gather.11.cloned.1.call-done = bf16[512,1536]{0,1:T(8,128)(2,1)} async-done(((bf16[128,1536]{0,1:T(8,128)(2,1)}), bf16[512,1536]{0,1:T(8,128)(2,1)}) %all-gather.11.cloned.1.call-update) | async-done | bytes 1572880 | tf_op jit(solution)/shard_map/all_gather | solution.py:173
  32.7 2.9 fusion.22
  35.6 3.7 %copy.100 = bf16[1,3,7,28,512]{3,2,1,0,4:T(8,128)(2,1)S(1)} copy(bf16[1,3,7,28,512]{4,3,1,2,0:T(8,128)(2,1)} %fusion.22) | data formatting | bytes 1204224 | tf_op jit(solution)/shard_map/convert_element_type | solution.py:203
  39.4 4.6 %reshape.410 = bf16[8,2,18816]{2,1,0:T(2,128)(2,1)} reshape(bf16[512,1,3,7,28]{4,3,2,1,0:T(8,128)(2,1)S(1)} %bitcast.241) | data formatting | bytes 1204224
  44.0 5.6 %all-to-all-start = ((bf16[8,2,18816]{2,1,0:T(2,128)(2,1)}), bf16[8,2,18816]{2,1,0:T(2,128)(2,1)}, u32[]{:S(2)}, u32[]{:S(2)}) async-start(bf16[8,2,18816]{2,1,0:T(2,128)(2,1)} %reshape.410), calls=%async_computation | async-start | bytes 1204224 | tf_op jit(solution)/shard_map/all_to_all | solution.py:204
  50.4 5.4 %all-gather.3 = bf16[4,4,169]{2,1,0:T(4,128)(2,1)S(1)} all-gather(bf16[1,4,169]{2,1,0:T(4,128)(2,1)S(1)} %bitcast.274), channel_id=1, replica_groups=mesh['fsdp'=4,'seq'=8] {'fsdp'}, dimensions={0}, use_global_device_ids=true | all-gather | bytes 6760 | tf_op jit(solution)/shard_map/all_gather | solution.py:175
  58.4 7.9 %all-to-all-done = bf16[8,2,18816]{2,1,0:T(2,128)(2,1)} async-done(((bf16[8,2,18816]{2,1,0:T(2,128)(2,1)}), bf16[8,2,18816]{2,1,0:T(2,128)(2,1)}, u32[]{:S(2)}, u32[]{:S(2)}) %all-to-all-start) | async-done | bytes 602144 | tf_op jit(solution)/shard_map/all_to_all | solution.py:204
  66.3 5.0 %reshape.411 = bf16[512,1,3,7,28]{4,3,2,1,0:T(8,128)(2,1)S(1)} reshape(bf16[8,2,18816]{2,1,0:T(2,128)(2,1)} %all-to-all-done) | data formatting | bytes 1204224
  71.3 4.5 %copy.101 = bf16[1,3,7,28,8,64]{5,2,4,3,1,0:T(8,128)(2,1)} copy(bf16[1,3,7,28,8,64]{3,2,1,5,4,0:T(8,128)(2,1)S(1)} %bitcast.240) | data formatting | bytes 1204224 | tf_op jit(solution)/shard_map/all_to_all | solution.py:204
  75.8 2.4 all_to_all.51
  80.4 4.3 %reshape.357 = bf16[1,3,8,7,4,7,2,32]{7,6,3,2,5,4,1,0:T(2,128)(2,1)S(1)} reshape(bf16[1,3,56,28,64]{4,2,3,1,0:T(8,128)(2,1)} %fusion.27) | data formatting | bytes 1204224 | tf_op jit(solution)/shard_map/reshape | solution.py:42
  98.7 3.7 %all-to-all-start.1 = ((bf16[8,2,6272]{2,1,0:T(2,128)(2,1)}), bf16[8,2,6272]{2,1,0:T(2,128)(2,1)S(1)}, u32[]{:S(2)}, u32[]{:S(2)}) async-start(bf16[8,2,6272]{2,1,0:T(2,128)(2,1)} %reshape.412), calls=%async_computation.1 | async-start | bytes 401408 | tf_op jit(solution)/shard_map/all_to_all | solution.py:212
  102.4 5.1 %all-gather.4 = bf16[4,1,128]{2,1,0:T(2,128)(2,1)S(1)} all-gather(bf16[1,1,128]{2,1,0:T(2,128)(2,1)S(1)} %bitcast.279), channel_id=1, replica_groups=mesh['fsdp'=4,'seq'=8] {'fsdp'}, dimensions={0}, use_global_device_ids=true | all-gather | bytes 1280 | tf_op jit(solution)/shard_map/all_gather | solution.py:176
  107.4 5.0 %all-gather.5 = bf16[4,1,128]{2,1,0:T(2,128)(2,1)S(1)} all-gather(bf16[1,1,128]{2,1,0:T(2,128)(2,1)S(1)} %bitcast.280), channel_id=1, replica_groups=mesh['fsdp'=4,'seq'=8] {'fsdp'}, dimensions={0}, use_global_device_ids=true | all-gather | bytes 1280 | tf_op jit(solution)/shard_map/all_gather | solution.py:177
  112.5 7.9 %all_gather.37 = bf16[512,512]{1,0:T(8,128)(2,1)S(1)} all-gather(bf16[128,512]{1,0:T(8,128)(2,1)S(1)} %copy-done.22), channel_id=1, replica_groups=mesh['fsdp'=4,'seq'=8] {'fsdp'}, dimensions={0}, use_global_device_ids=true | all-gather | bytes 655360 | tf_op jit(solution)/shard_map/all_gather | solution.py:174
  121.9 4.0 %multiply_convert_fusion = (bf16[7,28,2048]{2,1,0:T(8,128)(2,1)}, f32[7,28,2048]{2,1,0:T(8,128)}) fusion(bf16[512,2048]{1,0:T(8,128)(2,1)} %all-gather.13.cloned.1.call-done, f32[1,7,28,512]{3,2,1,0:T(8,128)S(1)} %get-tuple-element.84, f32[512]{0:T(512)S(1)} %bitcast.272, f32[512]{0:T(512)S(1)} %bitcast.262, f32[7,28]{1,0:T(8,128)S(1)} %add_rsqrt_fusion, ...), kind=kOutput, calls=%fused_computation.25 | convolution fusion | flops 413550592 | bytes 4912672 | tf_op jit(solution)/shard_map/brwc,cf->brwf/dot_general | solution.py:218
  125.9 3.3 fusion.3
  132.7 3.4 bitcast_convert_fusion.1
  137.0 3.3 bitcast_convert_fusion
  145.0 5.9 %all-to-all-start.2 = ((bf16[8,2,6272]{2,1,0:T(2,128)(2,1)}), bf16[8,2,6272]{2,1,0:T(2,128)(2,1)S(1)}, u32[]{:S(2)}, u32[]{:S(2)}) async-start(bf16[8,2,6272]{2,1,0:T(2,128)(2,1)} %reshape.414), calls=%async_computation.2 | async-start | bytes 401408 | tf_op jit(solution)/shard_map/all_to_all | solution.py:249
  152.6 6.9 %all-to-all-done.2 = bf16[8,2,6272]{2,1,0:T(2,128)(2,1)S(1)} async-done(((bf16[8,2,6272]{2,1,0:T(2,128)(2,1)}), bf16[8,2,6272]{2,1,0:T(2,128)(2,1)S(1)}, u32[]{:S(2)}, u32[]{:S(2)}) %all-to-all-start.2) | async-done | bytes 200736 | tf_op jit(solution)/shard_map/all_to_all | solution.py:249
  168.7 2.4 copy.126
  185.6 19.8 %all_to_all.66 = bf16[8,2,18816]{2,1,0:T(2,128)(2,1)S(1)} all-to-all(bf16[8,2,18816]{2,1,0:T(2,128)(2,1)S(1)} %reshape.416), channel_id=1, replica_groups=mesh['fsdp'=4,'seq'=8] {'seq'}, dimensions={0} | all-to-all | bytes 1204224 | tf_op jit(solution)/shard_map/all_to_all | solution.py:255
  213.1 3.0 fusion.32
  216.2 5.8 %reduce-scatter.11.cloned.1.call-done = bf16[512,512]{1,0:T(8,128)(2,1)} async-done(((bf16[2048,512]{1,0:T(8,128)(2,1)}), bf16[512,512]{1,0:T(8,128)(2,1)}) %reduce-scatter.11.cloned.1.call-update) | async-done | bytes 524304 | tf_op jit(solution)/shard_map/reduce_scatter | solution.py:293
  222.1 30.6 %reduce-scatter.5.cloned.1.call-done = bf16[128,1536]{1,0:T(8,128)(2,1)} async-done(((bf16[512,1536]{1,0:T(8,128)(2,1)}), bf16[128,1536]{1,0:T(8,128)(2,1)}) %reduce-scatter.5.cloned.1.call-update) | async-done | bytes 393232 | tf_op jit(solution)/shard_map/reduce_scatter | solution.py:275
  256.0 10.1 %all-reduce.7 = (bf16[512]{0:T(512)(128)(2,1)S(1)}, bf16[512]{0:T(512)(128)(2,1)S(1)}, bf16[16,169]{1,0:T(8,128)(2,1)S(1)}, bf16[512]{0:T(512)(128)(2,1)S(1)}, bf16[512]{0:T(512)(128)(2,1)S(1)}) all-reduce(bf16[512]{0:T(512)(128)(2,1)S(1)} %get-tuple-element.57, ...), channel_id=3, replica_groups=mesh['fsdp'=4,'seq'=8] {'fsdp'}, use_global_device_ids=true, to_apply=%region_11.12.clone | all-reduce | flops 4752 | bytes 19008
  266.4 22.5 %all-reduce.5 = (bf16[128]{0:T(256)(128)(2,1)S(1)}, bf16[4,169]{1,0:T(4,128)(2,1)S(1)}, bf16[128]{0:T(256)(128)(2,1)S(1)}, bf16[128]{0:T(256)(128)(2,1)S(1)}) all-reduce(bf16[128]{0:T(256)(128)(2,1)S(1)} %dynamic-slice.3, bf16[4,169]{1,0:T(4,128)(2,1)S(1)} %constant_dynamic-slice_fusion, ...), channel_id=1, replica_groups=mesh['fsdp'=4,'seq'=8] {'seq'}, use_global_device_ids=true, to_apply=%region_15.16 | all-reduce | flops 1060 | bytes 4240 | tf_op jit(solution)/shard_map/psum | solution.py:299
  290.5 16.3 %all-gather.6 = bf16[8,1,128]{2,1,0:T(2,128)(2,1)S(1)} all-gather(bf16[1,1,128]{2,1,0:T(2,128)(2,1)S(1)} %dynamic-slice_bitcast_fusion), channel_id=2, replica_groups=mesh['fsdp'=4,'seq'=8] {'seq'}, dimensions={0}, use_global_device_ids=true | all-gather | bytes 2304 | tf_op jit(solution)/shard_map/all_gather | solution.py:298
  309.4 36.9 %all-reduce.10.cloned.1.call-done = (bf16[128,1536]{1,0:T(8,128)(2,1)}, bf16[128,512]{1,0:T(8,128)(2,1)}, bf16[128,2048]{1,0:T(8,128)(2,1)}, bf16[512,512]{1,0:T(8,128)(2,1)}) async-done(((bf16[128,1536]{1,0:T(8,128)(2,1)}, bf16[128,512]{1,0:T(8,128)(2,1)}, bf16[128,2048]{1,0:T(8,128)(2,1)}, bf16[512,512]{1,0:T(8,128)(2,1)}), (bf16[128,1536]{1,0:T(8,128)(2,1)}, bf16[128,512]{1,0:T(8,128)(2,1)}, ...) | async-done | bytes 1572880 | tf_op jit(solution)/shard_map/psum | solution.py:300
  (204 shorter events, 78.1 us)
Async XLA Ops:
  7.2 25.5 %copy-start.34 = (f32[3]{0:T(128)S(1)}, f32[3]{0:T(128)}, u32[]{:S(2)}) copy-start(f32[3]{0:T(128)} %constant.43.clone) | copy-start | bytes 40
  7.2 14.5 %copy-start.7 = (bf16[1,7,28,512]{3,2,1,0:T(8,128)(2,1)S(1)}, bf16[1,7,28,512]{3,2,1,0:T(8,128)(2,1)}, u32[]{:S(2)}) copy-start(bf16[1,7,28,512]{3,2,1,0:T(8,128)(2,1)} %param.14) | copy-start | bytes 602116
  7.2 25.5 %all-gather.11.cloned.1.call-start = ((), (), s32[]{:S(2)}) async-start(), calls=%async_computation.8 | async-start | bytes 1966080 | tf_op jit(solution)/shard_map/all_gather | solution.py:173
  9.2 112.7 %all-gather.13.cloned.1.call-start = ((), (), s32[]{:S(2)}) async-start(), calls=%async_computation.9 | async-start | bytes 2621440 | tf_op jit(solution)/shard_map/all_gather | solution.py:178
  21.6 11.1 %copy-start.26 = (f32[4,1,128]{2,1,0:T(1,128)}, f32[4,1,128]{2,1,0:T(1,128)S(1)}, u32[]{:S(2)}) copy-start(f32[4,1,128]{2,1,0:T(1,128)S(1)} %convert_element_type.192) | copy-start | bytes 6148
  39.4 11.0 %copy-start.25 = (bf16[4,169]{1,0:T(4,128)(2,1)S(1)}, bf16[4,169]{1,0:T(4,128)(2,1)}, u32[]{:S(2)}) copy-start(bf16[4,169]{1,0:T(4,128)(2,1)} %param.22) | copy-start | bytes 4060
  39.4 16.4 %copy-start.31 = (s32[49,49]{1,0:T(8,128)S(1)}, s32[49,49]{1,0:T(8,128)}, u32[]{:S(2)}) copy-start(s32[49,49]{1,0:T(8,128)} %param.17) | copy-start | bytes 28816
  44.0 12.7 %copy-start.23 = (s32[56,28]{0,1:T(8,128)S(1)}, s32[56,28]{0,1:T(8,128)}, u32[]{:S(2)}) copy-start(s32[56,28]{0,1:T(8,128)} %param.16) | copy-start | bytes 18820
  44.0 22.3 %all-to-all-start = ((bf16[8,2,18816]{2,1,0:T(2,128)(2,1)}), bf16[8,2,18816]{2,1,0:T(2,128)(2,1)}, u32[]{:S(2)}, u32[]{:S(2)}) async-start(bf16[8,2,18816]{2,1,0:T(2,128)(2,1)} %reshape.410), calls=%async_computation | async-start | bytes 1204224 | tf_op jit(solution)/shard_map/all_to_all | solution.py:204
  49.6 76.3 %all-gather.15.cloned.1.call-start = ((), (), s32[]{:S(2)}) async-start(), calls=%async_computation.10 | async-start | bytes 2621440 | tf_op jit(solution)/shard_map/all_gather | solution.py:179
  87.3 2.9 copy-start.2
  97.4 5.0 %copy-start.29 = (bf16[128]{0:T(256)(128)(2,1)S(1)}, bf16[128]{0:T(256)(128)(2,1)}, u32[]{:S(2)}) copy-start(bf16[128]{0:T(256)(128)(2,1)} %param.23) | copy-start | bytes 772
  97.4 10.1 %copy-start.30 = (bf16[128]{0:T(256)(128)(2,1)S(1)}, bf16[128]{0:T(256)(128)(2,1)}, u32[]{:S(2)}) copy-start(bf16[128]{0:T(256)(128)(2,1)} %param.24) | copy-start | bytes 772
  97.4 15.1 %copy-start.22 = (bf16[128,512]{1,0:T(8,128)(2,1)S(1)}, bf16[128,512]{1,0:T(8,128)(2,1)}, u32[]{:S(2)}) copy-start(bf16[128,512]{1,0:T(8,128)(2,1)} %param.21) | copy-start | bytes 393220
  98.7 21.8 %all-to-all-start.1 = ((bf16[8,2,6272]{2,1,0:T(2,128)(2,1)}), bf16[8,2,6272]{2,1,0:T(2,128)(2,1)S(1)}, u32[]{:S(2)}, u32[]{:S(2)}) async-start(bf16[8,2,6272]{2,1,0:T(2,128)(2,1)} %reshape.412), calls=%async_computation.1 | async-start | bytes 401408 | tf_op jit(solution)/shard_map/all_to_all | solution.py:212
  102.3 113.9 %reduce-scatter.7.cloned.1.call-start = ((), (), s32[]{:S(2)}) async-start(), calls=%async_computation.12 | async-start | bytes 655360 | tf_op jit(solution)/shard_map/reduce_scatter | solution.py:278
  112.5 8.8 %copy-start.8 = (bf16[1,7,28,512]{3,2,1,0:T(8,128)(2,1)S(1)}, bf16[1,7,28,512]{3,2,1,0:T(8,128)(2,1)}, u32[]{:S(2)}) copy-start(bf16[1,7,28,512]{3,2,1,0:T(8,128)(2,1)} %param.14) | copy-start | bytes 602116
  121.9 4.0 %copy-start.18 = (bf16[1,7,28,512]{3,2,1,0:T(8,128)(2,1)S(1)}, bf16[1,7,28,512]{3,2,1,0:T(8,128)(2,1)}, u32[]{:S(2)}) copy-start(bf16[1,7,28,512]{3,2,1,0:T(8,128)(2,1)} %param.15) | copy-start | bytes 602116
  125.9 3.3 copy-start.12
  131.5 8.8 %copy-start.4 = (f32[1,7,28,512]{3,2,1,0:T(8,128)}, f32[1,7,28,512]{3,2,1,0:T(8,128)S(1)}, u32[]{:S(2)}) copy-start(f32[1,7,28,512]{3,2,1,0:T(8,128)S(1)} %fusion.67) | copy-start | bytes 1204228
  132.7 83.6 %reduce-scatter.9.cloned.1.call-start = ((), (), s32[]{:S(2)}) async-start(), calls=%async_computation.13 | async-start | bytes 2621440 | tf_op jit(solution)/shard_map/reduce_scatter | solution.py:290
  136.1 86.0 %reduce-scatter.11.cloned.1.call-start = ((), (), s32[]{:S(2)}) async-start(), calls=%async_computation.14 | async-start | bytes 2621440 | tf_op jit(solution)/shard_map/reduce_scatter | solution.py:293
  145.0 14.5 %all-to-all-start.2 = ((bf16[8,2,6272]{2,1,0:T(2,128)(2,1)}), bf16[8,2,6272]{2,1,0:T(2,128)(2,1)S(1)}, u32[]{:S(2)}, u32[]{:S(2)}) async-start(bf16[8,2,6272]{2,1,0:T(2,128)(2,1)} %reshape.414), calls=%async_computation.2 | async-start | bytes 401408 | tf_op jit(solution)/shard_map/all_to_all | solution.py:249
  151.0 101.7 %reduce-scatter.5.cloned.1.call-start = ((), (), s32[]{:S(2)}) async-start(), calls=%async_computation.11 | async-start | bytes 1966080 | tf_op jit(solution)/shard_map/reduce_scatter | solution.py:275
  164.1 3.1 copy-start.15
  167.3 3.9 %copy-start.14 = (bf16[1,1,8,4,2,49,32]{5,6,4,3,2,1,0:T(8,128)(2,1)S(1)}, bf16[1,1,8,4,2,49,32]{5,6,4,3,2,1,0:T(8,128)(2,1)}, u32[]{:S(2)}) copy-start(bf16[1,1,8,4,2,49,32]{5,6,4,3,2,1,0:T(8,128)(2,1)} %copy.151) | copy-start | bytes 602116
  174.8 3.1 copy-start.10
  211.1 135.1 %all-reduce.10.cloned.1.call-start = ((), (), s32[]{:S(2)}) async-start(), calls=%async_computation.15 | async-start | bytes 3145728 | tf_op jit(solution)/shard_map/psum | solution.py:300
  213.1 39.6 %copy-start.32 = (s32[49,49]{1,0:T(8,128)S(1)}, s32[49,49]{1,0:T(8,128)}, u32[]{:S(2)}) copy-start(s32[49,49]{1,0:T(8,128)} %param.17) | copy-start | bytes 28816
  253.8 54.2 %copy-start.5 = (f32[1,7,28,512]{3,2,1,0:T(8,128)S(1)}, f32[1,7,28,512]{3,2,1,0:T(8,128)}, u32[]{:S(2)}) copy-start(f32[1,7,28,512]{3,2,1,0:T(8,128)} %copy-done.4) | copy-start | bytes 1204228
  346.2 3.7 %copy-start.17 = (bf16[128,2048]{1,0:T(8,128)(2,1)S(1)}, bf16[128,2048]{1,0:T(8,128)(2,1)}, u32[]{:S(2)}) copy-start(bf16[128,2048]{1,0:T(8,128)(2,1)} %get-tuple-element.69) | copy-start | bytes 1572868
  346.2 4.7 %copy-start.16 = (bf16[512,512]{1,0:T(8,128)(2,1)S(1)}, bf16[512,512]{1,0:T(8,128)(2,1)}, u32[]{:S(2)}) copy-start(bf16[512,512]{1,0:T(8,128)(2,1)} %get-tuple-element.70) | copy-start | bytes 1572868
  (17 other events, 28.6 us)
Sparse Core Ops, SparseCore 0:
  10.1 22.5 all-gather.10
  34.3 22.5 all-gather.12
  58.5 22.5 all-gather.14
  132.8 22.0 reduce-scatter.6
  157.3 31.1 reduce-scatter.8
  190.8 31.1 reduce-scatter.10
  224.6 28.0 reduce-scatter.4
  256.5 89.7 all-reduce.9
